TPU v7x, 256 devices: a whole 4x4x8 slice. The times are simulated.
256 devices in a mesh: pop: 32 (over x, y, core), site: 8 (over z).
Axes of the slice: x: 4, y: 4, z: 8, core: 2. Of those that a mesh axis runs over, the one named last changes fastest.
Arguments:
- profile: bfloat16 [32768, 96], P(('pop', 'site')), may hold values from 0 to 1
- panel: bfloat16 [32768, 128], P(('pop', 'site')), may hold values from -6 to 6
- visit_person: int32 [131072], P(('pop', 'site')), may hold values from 0 to 127
- visit_owner: int32 [131072], P(('pop', 'site')), may hold values from 0 to 31, as said below
- visit_row: int32 [131072], P(('pop', 'site')), may hold values from 0 to 1023, as said below
- visit_start: int32 [131072], P(('pop', 'site')), may hold values from 0 to 95
- visit_length: int32 [131072], P(('pop', 'site')), may hold values from 2 to 48
- tile_loc: int32 [2048], P(('pop', 'site')), may hold values from 0 to 7
Outputs:
- exposure: bfloat16 [32768, 128], P(('pop', 'site'))
Inputs may be any that keep to these rules, and one draw needn't show every extreme that they name: `visit_owner`: all devices with one site index send the same number of visits to a given owner index; at most 24 visits of one device go to one owner index, and in every draw some owner index receives exactly 24 from every device of a site index. `visit_row`: among the visits that reach one owner device the rows are distinct; in each tile the rows that are used come first and the rest are empty.
All inputs are finite; a program needn't handle non-finite values.
Results may differ from a plain program's by a relative error of at most 0.013.
Values may be sent and summed in bfloat16 or wider, within the bound.
No kernel may reach another device: no remote copies, remote signals or barrier semaphores. Data moves between devices by JAX's collectives and lax.ppermute only.
A program may use at most 64 MiB of HBM per device.

v0:
```python
import math
import jax
import jax.numpy as jnp
from jax import lax
from jax.sharding import PartitionSpec as P


def pair_terms(own_weights, own_places, running, pieces):
    far_weights, far_panel, far_places = pieces
    piece_tiles = far_weights.shape[0]
    group_size = math.gcd(piece_tiles, 8)
    group_count = piece_tiles // group_size
    grouped = (
        far_weights.reshape((group_count, group_size) + far_weights.shape[1:]),
        far_panel.reshape((group_count, group_size) + far_panel.shape[1:]),
        far_places.reshape(group_count, group_size),
    )

    def one_group(carried, item):
        group_weights, group_panel, group_places = item
        same_place = (own_places[:, None] == group_places[None, :]).astype(jnp.bfloat16)
        masked_far = group_weights[None, :, :, :] * same_place[:, :, None, None]
        copresence = jnp.einsum(
            "ars,abqs->abrq", own_weights, masked_far, preferred_element_type=jnp.float32
        )
        high_part = copresence.astype(jnp.bfloat16)
        low_part = (copresence - high_part.astype(jnp.float32)).astype(jnp.bfloat16)
        added = jnp.einsum(
            "abrq,bqc->arc", high_part, group_panel, preferred_element_type=jnp.float32
        )
        added = added + jnp.einsum(
            "abrq,bqc->arc", low_part, group_panel, preferred_element_type=jnp.float32
        )
        return (carried + added, None)

    result_sum, unused = lax.scan(one_group, running, grouped)
    return result_sum


def per_device(
    profile, panel, visit_person, visit_owner, visit_row, visit_start, visit_length, tile_loc
):
    pop_count = lax.axis_size("pop")
    visit_count = visit_person.shape[0]
    person_count, slot_count = profile.shape
    panel_width = panel.shape[1]
    capacity = visit_count // pop_count * 3 // 2
    tile_count = tile_loc.shape[0]
    row_count = tile_count * 128
    slot_ids = jnp.arange(slot_count, dtype=jnp.int32)
    finish = jnp.minimum(visit_start + visit_length, slot_count)
    inside = (slot_ids[None, :] >= visit_start[:, None]) & (slot_ids[None, :] < finish[:, None])
    weights = jnp.where(inside, profile[visit_person], jnp.zeros((), jnp.bfloat16))
    visit_panel = panel[visit_person]
    owner_hot = (visit_owner[:, None] == jnp.arange(pop_count, dtype=jnp.int32)[None, :]).astype(
        jnp.int32
    )
    position = jnp.sum((jnp.cumsum(owner_hot, axis=0) - 1) * owner_hot, axis=1)
    send_index = visit_owner * capacity + position
    send_weights = (
        jnp.zeros((pop_count * capacity, slot_count), jnp.bfloat16)
        .at[send_index]
        .set(weights)
        .reshape(pop_count, capacity, slot_count)
    )
    send_panel = (
        jnp.zeros((pop_count * capacity, panel_width), jnp.bfloat16)
        .at[send_index]
        .set(visit_panel)
        .reshape(pop_count, capacity, panel_width)
    )
    send_rows = (
        jnp.full((pop_count * capacity,), row_count, jnp.int32)
        .at[send_index]
        .set(visit_row)
        .reshape(pop_count, capacity)
    )
    got_weights, got_panel, got_rows = (
        lax.all_to_all(send_weights, "pop", split_axis=0, concat_axis=0, tiled=True),
        lax.all_to_all(send_panel, "pop", split_axis=0, concat_axis=0, tiled=True),
        lax.all_to_all(send_rows, "pop", split_axis=0, concat_axis=0, tiled=True),
    )
    target = got_rows.reshape(-1)
    tile_weights = (
        jnp.zeros((row_count, slot_count), jnp.bfloat16)
        .at[target]
        .set(got_weights.reshape(-1, slot_count), mode="drop")
        .reshape(tile_count, 128, slot_count)
    )
    tile_panel = (
        jnp.zeros((row_count, panel_width), jnp.bfloat16)
        .at[target]
        .set(got_panel.reshape(-1, panel_width), mode="drop")
        .reshape(tile_count, 128, panel_width)
    )
    initial = jnp.zeros((tile_count, 128, panel_width), jnp.float32)
    summed_rows = pair_terms(
        tile_weights,
        tile_loc,
        initial,
        (
            lax.all_gather(tile_weights, "site", axis=0, tiled=True),
            lax.all_gather(tile_panel, "site", axis=0, tiled=True),
            lax.all_gather(tile_loc, "site", axis=0, tiled=True),
        ),
    )
    row_result = (summed_rows / slot_count).astype(jnp.bfloat16).reshape(row_count, panel_width)
    sent_back = row_result[jnp.minimum(got_rows, row_count - 1)]
    returned = lax.all_to_all(sent_back, "pop", split_axis=0, concat_axis=0, tiled=True)
    own_results = returned.reshape(pop_count * capacity, panel_width)[send_index]
    person_hot = (
        jnp.arange(person_count, dtype=jnp.int32)[:, None] == visit_person[None, :]
    ).astype(jnp.bfloat16)
    return jnp.dot(person_hot, own_results, preferred_element_type=jnp.float32).astype(jnp.bfloat16)


def solution(mesh):
    placed = (
        P(("pop", "site"), None),
        P(("pop", "site"), None),
        P(("pop", "site")),
        P(("pop", "site")),
        P(("pop", "site")),
        P(("pop", "site")),
        P(("pop", "site")),
        P(("pop", "site")),
    )
    return jax.shard_map(
        per_device, mesh=mesh, in_specs=placed, out_specs=P(("pop", "site"), None), check_vma=False
    )
```

profile of v0, /device:TPU:1, one launch (start us, length us, event | category | flops | bytes accessed | tf_op | source)
XLA Modules:
  0.0 205.3 jit_solution(10561987336551839992)
XLA Ops:
  7.2 1.2 reduce-window.6
  10.2 2.6 %scatter_custom_fusion = s32[768]{0:T(1024)S(1)} fusion(s32[512]{0:T(512)S(1)} %get-tuple-element.104, s32[512]{0:T(512)} %param.14, s32[]{:T(128)} %constant.8.clone.1), kind=kCustom, calls=%fused_computation.71 | custom fusion | bytes 3584 | tf_op jit(solution)/shard_map/scatter | solution.py:75
  13.5 8.6 %all-to-all-start = ((s32[32,1,24]{2,1,0:T(1,128)}), s32[32,1,24]{2,1,0:T(1,128)S(1)}, u32[]{:S(2)}, u32[]{:S(2)}) async-start(s32[32,1,24]{2,1,0:T(1,128)} %bitcast.2), calls=%async_computation | async-start | bytes 32768 | tf_op jit(solution)/shard_map/all_to_all | solution.py:81
  23.6 3.9 %scatter_custom_fusion.1 = bf16[768,96]{1,0:T(8,128)(2,1)} fusion(s32[512]{0:T(512)S(1)} %get-tuple-element.104, s32[512]{0:T(512)S(1)} %get-tuple-element.105, s32[512]{0:T(512)} %param.15, bf16[]{:T(256)} %constant.19.clone.1, bf16[128,96]{1,0:T(8,128)(2,1)S(1)} %copy.29, s32[1024]{0:T(1024)S(1)} %pad_clamp_fusion.2), kind=kCustom, calls=%fused_computation.40 | custom fusion | flops 196608 | bytes 189440 | tf_op jit(solution)/shard_map/scatter | solution.py:63
  27.5 1.4 all-to-all-done
  28.9 6.0 %all-to-all-start.1 = ((bf16[32,24,96]{2,1,0:T(8,128)(2,1)}), bf16[32,24,96]{2,1,0:T(8,128)(2,1)S(1)}, u32[]{:S(2)}, u32[]{:S(2)}) async-start(bf16[32,24,96]{2,1,0:T(8,128)(2,1)} %bitcast.3), calls=%async_computation.1 | async-start | bytes 393216 | tf_op jit(solution)/shard_map/all_to_all | solution.py:79
  36.3 7.0 %all-to-all-done.1 = bf16[32,24,96]{2,1,0:T(8,128)(2,1)S(1)} async-done(((bf16[32,24,96]{2,1,0:T(8,128)(2,1)}), bf16[32,24,96]{2,1,0:T(8,128)(2,1)S(1)}, u32[]{:S(2)}, u32[]{:S(2)}) %all-to-all-start.1) | async-done | bytes 147488 | tf_op jit(solution)/shard_map/all_to_all | solution.py:79
  43.2 4.3 %scatter_custom_fusion.2 = bf16[1024,96]{1,0:T(8,128)(2,1)S(1)} fusion(s32[768]{0:T(1024)S(1)} %fusion.39, bf16[768,96]{1,0:T(8,128)(2,1)S(1)} %bitcast.114, bf16[]{:T(256)} %constant.19.clone.1), kind=kCustom, calls=%fused_computation.47 | custom fusion | bytes 196610 | tf_op jit(solution)/shard_map/scatter | solution.py:87
  48.5 3.0 %scatter_custom_fusion.3 = bf16[768,128]{1,0:T(8,128)(2,1)S(1)} fusion(s32[512]{0:T(512)S(1)} %get-tuple-element.104, bf16[128,128]{1,0:T(8,128)(2,1)S(1)} %copy-done, s32[1024]{0:T(1024)S(1)} %pad_clamp_fusion.2, bf16[]{:T(256)} %constant.19.clone.1), kind=kCustom, calls=%fused_computation.41 | custom fusion | bytes 196610 | tf_op jit(solution)/shard_map/scatter | solution.py:69
  51.5 11.9 %all_to_all.24 = bf16[32,24,128]{2,1,0:T(8,128)(2,1)S(1)} all-to-all(bf16[32,24,128]{2,1,0:T(8,128)(2,1)S(1)} %bitcast.112), channel_id=1, replica_groups=mesh['pop'=32,'site'=8] {'pop'}, dimensions={0} | all-to-all | bytes 393216 | tf_op jit(solution)/shard_map/all_to_all | solution.py:80
  63.4 4.9 %scatter_custom_fusion.4 = bf16[1024,128]{1,0:T(8,128)(2,1)} fusion(s32[768]{0:T(1024)S(1)} %fusion.39, bf16[768,128]{1,0:T(8,128)(2,1)S(1)} %bitcast.115, bf16[]{:T(256)} %constant.19.clone.1), kind=kCustom, calls=%fused_computation.43 | custom fusion | bytes 262146 | tf_op jit(solution)/shard_map/scatter | solution.py:93
  69.9 13.6 %all-reduce = s32[64]{0:T(128)S(1)} all-reduce(s32[64]{0:T(128)S(1)} %dynamic-update-slice), channel_id=1, replica_groups=mesh['pop'=32,'site'=8] {'site'}, use_global_device_ids=true, to_apply=%add | all-reduce | flops 64 | bytes 512
  83.9 3.5 %all-gather.3.cloned.1.call-done = bf16[64,128,96]{1,0,2:T(8,128)(2,1)} async-done(((bf16[8,128,96]{1,0,2:T(8,128)(2,1)}), bf16[64,128,96]{1,0,2:T(8,128)(2,1)}) %all-gather.3.cloned.1.call-update) | async-done | bytes 1572880 | tf_op jit(solution)/shard_map/all_gather | solution.py:102
  87.3 42.4 %all-gather.5.cloned.1.call-done = bf16[64,128,128]{2,1,0:T(8,128)(2,1)} async-done(((bf16[8,128,128]{2,1,0:T(8,128)(2,1)}), bf16[64,128,128]{2,1,0:T(8,128)(2,1)}) %all-gather.5.cloned.1.call-update) | async-done | bytes 2097168 | tf_op jit(solution)/shard_map/all_gather | solution.py:103
  129.7 44.4 %while.11 = (s32[]{:T(128)}, f32[8,128,128]{2,1,0:T(8,128)S(1)}, bf16[8,8,128,96]{2,1,0,3:T(8,128)(2,1)}, s32[8]{0:T(128)S(1)}, s32[8,8]{1,0:T(8,128)S(1)}, /*in...) while((s32[]{:T(128)}, f32[8,128,128]{2,1,0:T(8,128)S(1)}, ...), condition=%wide.region_9.10_spmd.clone, body=%wide.region_8.9_spmd.clone.sunk | while | flops 743571584 | bytes 16384511 | solution.py:36
  129.8 0.9 constant_dynamic-slice_fusion.3
  130.8 0.9 fusion.66
  131.7 1.7 fusion.67
  133.4 1.9 fusion.68
  135.4 0.9 constant_dynamic-slice_fusion.3
  136.3 0.9 fusion.66
  137.3 1.7 fusion.67
  139.0 1.9 fusion.68
  140.9 0.9 constant_dynamic-slice_fusion.3
  141.9 0.9 fusion.66
  142.8 1.7 fusion.67
  144.5 1.9 fusion.68
  146.5 0.9 constant_dynamic-slice_fusion.3
  147.5 0.9 fusion.66
  148.4 1.7 fusion.67
  150.1 1.9 fusion.68
  152.0 0.9 constant_dynamic-slice_fusion.3
  153.0 0.9 fusion.66
  153.9 1.7 fusion.67
  155.6 1.9 fusion.68
  157.6 0.9 constant_dynamic-slice_fusion.3
  159.5 1.7 fusion.67
  161.2 1.9 fusion.68
  163.2 0.9 constant_dynamic-slice_fusion.3
  165.0 1.7 fusion.67
  166.7 1.9 fusion.68
  168.7 0.9 constant_dynamic-slice_fusion.3
  170.6 1.7 fusion.67
  172.3 1.9 fusion.68
  174.3 2.5 %gather_fusion = bf16[768,128]{1,0:T(8,128)(2,1)} fusion(bf16[1024,128]{1,0:T(8,128)(2,1)S(1)} %bitcast.106, s32[1024]{0:T(1024)S(1)} %pad_clamp_fusion.1), kind=kCustom, calls=%fused_computation.2 | custom fusion | bytes 396288 | tf_op jit(solution)/shard_map/gather | solution.py:108
  176.8 11.2 %all-to-all-start.3 = ((bf16[32,24,128]{2,1,0:T(8,128)(2,1)}), bf16[32,24,128]{2,1,0:T(8,128)(2,1)S(1)}, u32[]{:S(2)}, u32[]{:S(2)}) async-start(bf16[32,24,128]{2,1,0:T(8,128)(2,1)} %bitcast.14), calls=%async_computation.3 | async-start | bytes 393216 | tf_op jit(solution)/shard_map/all_to_all | solution.py:109
  188.0 8.3 %all-to-all-done.3 = bf16[32,24,128]{2,1,0:T(8,128)(2,1)S(1)} async-done(((bf16[32,24,128]{2,1,0:T(8,128)(2,1)}), bf16[32,24,128]{2,1,0:T(8,128)(2,1)S(1)}, u32[]{:S(2)}, u32[]{:S(2)}) %all-to-all-start.3) | async-done | bytes 196640 | tf_op jit(solution)/shard_map/all_to_all | solution.py:109
  196.4 1.3 gather_fusion.1
  (66 shorter events, 12.6 us)
Async XLA Ops:
  6.5 41.9 %copy-start = (bf16[128,128]{1,0:T(8,128)(2,1)S(1)}, bf16[128,128]{1,0:T(8,128)(2,1)}, u32[]{:S(2)}) copy-start(bf16[128,128]{1,0:T(8,128)(2,1)} %param.11) | copy-start | bytes 98308
  6.5 61.8 %copy-start.3 = (u32[256]{0:T(256)S(1)}, u32[256]{0:T(256)}, u32[]{:S(2)}) copy-start(u32[256]{0:T(256)} %constant.52) | copy-start | bytes 3076
  6.5 63.1 %copy-start.1 = (s32[8]{0:T(128)S(1)}, s32[8]{0:T(128)}, u32[]{:S(2)}) copy-start(s32[8]{0:T(128)} %param.17) | copy-start | bytes 100
  13.5 15.5 %all-to-all-start = ((s32[32,1,24]{2,1,0:T(1,128)}), s32[32,1,24]{2,1,0:T(1,128)S(1)}, u32[]{:S(2)}, u32[]{:S(2)}) async-start(s32[32,1,24]{2,1,0:T(1,128)} %bitcast.2), calls=%async_computation | async-start | bytes 32768 | tf_op jit(solution)/shard_map/all_to_all | solution.py:81
  28.9 14.3 %all-to-all-start.1 = ((bf16[32,24,96]{2,1,0:T(8,128)(2,1)}), bf16[32,24,96]{2,1,0:T(8,128)(2,1)S(1)}, u32[]{:S(2)}, u32[]{:S(2)}) async-start(bf16[32,24,96]{2,1,0:T(8,128)(2,1)} %bitcast.3), calls=%async_computation.1 | async-start | bytes 393216 | tf_op jit(solution)/shard_map/all_to_all | solution.py:79
  34.9 52.4 %all-gather.3.cloned.1.call-start = ((), (), s32[]{:S(2)}) async-start(), calls=%async_computation.4 | async-start | bytes 1769472 | tf_op jit(solution)/shard_map/all_gather | solution.py:102
  48.4 81.3 %all-gather.5.cloned.1.call-start = ((), (), s32[]{:S(2)}) async-start(), calls=%async_computation.5 | async-start | bytes 2359296 | tf_op jit(solution)/shard_map/all_gather | solution.py:103
  174.2 23.5 %copy-start.2 = (s32[512]{0:T(512)S(1)}, s32[512]{0:T(512)}, u32[]{:S(2)}) copy-start(s32[512]{0:T(512)} %param.12) | copy-start | bytes 6148
  176.8 19.6 %all-to-all-start.3 = ((bf16[32,24,128]{2,1,0:T(8,128)(2,1)}), bf16[32,24,128]{2,1,0:T(8,128)(2,1)S(1)}, u32[]{:S(2)}, u32[]{:S(2)}) async-start(bf16[32,24,128]{2,1,0:T(8,128)(2,1)} %bitcast.14), calls=%async_computation.3 | async-start | bytes 393216 | tf_op jit(solution)/shard_map/all_to_all | solution.py:109
Sparse Core Ops, SparseCore 0:
  48.5 38.7 all-gather.2
  89.1 40.5 all-gather.4
where the time goes:
time: 207 us; the launch traced here: 205 us
  waiting for transfers between devices  62.6 us (30%)
  matrix products  36.5 us (18%)
  local copies, waits for them, and re-layouts  30.9 us (15%)
  starting transfers between devices  25.9 us (13%)
  blocking collectives  25.5 us (12%)
  between operations  14.2 us (7%)
  other arithmetic  9.37 us (5%)
    all_gather x1, waiting for transfers between devices, per_device(): lax.all_gather(tile_panel, 'site', axis=0, tiled=True)  42.4 us
    dot_general x8, matrix products, one_group(): jnp.einsum('abrq,bqc->arc', high_part, group_panel, preferred_element_typ...  14.8 us
    unnamed x1, blocking collectives  13.6 us
    dot_general x8, matrix products, one_group(): jnp.einsum('abrq,bqc->arc', low_part, group_panel, preferred_element_type...  13.6 us
    all_to_all x1, blocking collectives, per_device(): lax.all_to_all(send_panel, 'pop', split_axis=0, concat_axis=0, tiled=True)  11.9 us
    all_to_all x1, starting transfers between devices, per_device(): lax.all_to_all(sent_back, 'pop', split_axis=0, concat_axis=0, tiled=True)  11.2 us
    all_to_all x1, starting transfers between devices, per_device(): lax.all_to_all(send_rows, 'pop', split_axis=0, concat_axis=0, tiled=True)  8.59 us
    all_to_all x1, waiting for transfers between devices, per_device(): lax.all_to_all(sent_back, 'pop', split_axis=0, concat_axis=0, tiled=True)  8.32 us
  transfers between devices with their start and end apart: 5, of which 5 were waited for; matrix products, arithmetic and copies ran while one was open for 8% of the time, Pallas kernels for 0%

commit v1 on v0

--- a/solution.py
+++ b/solution.py
@@ -3,6 +3,11 @@
 import jax.numpy as jnp
 from jax import lax
 from jax.sharding import PartitionSpec as P
+
+
+def gather_by_exchange(array, axis, dim):
+    copies = jnp.concatenate([array] * lax.axis_size(axis), axis=dim)
+    return lax.all_to_all(copies, axis, dim, dim, tiled=True)
 
 
 def pair_terms(own_weights, own_places, running, pieces):
@@ -100,7 +105,7 @@
         initial,
         (
             lax.all_gather(tile_weights, "site", axis=0, tiled=True),
-            lax.all_gather(tile_panel, "site", axis=0, tiled=True),
+            gather_by_exchange(tile_panel, "site", 0),
             lax.all_gather(tile_loc, "site", axis=0, tiled=True),
         ),
     )

time: 207 us -> 228 us (1.10)
  waiting for transfers between devices: 62.6 us -> 29.5 us
  blocking collectives: 25.5 us -> 53.4 us
  local copies, waits for them, and re-layouts: 30.9 us -> 47.9 us
  starting transfers between devices: 25.9 us -> 33 us
    all_gather x1 -> x0, waiting for transfers between devices: 42.4 us -> none  [per_device(): lax.all_gather(tile_panel, 'site', axis=0, tiled=True)]
    unnamed x1, blocking collectives: 13.6 us -> 53.4 us
    while x0 -> x16, local copies, waits for them, and re-layouts: none -> 15.3 us
    all_to_all x0 -> x2, starting transfers between devices: none -> 12.4 us  [the longest x1 8.19 us: gather_by_exchange(): return lax.all_to_all(copies, axis, dim, dim, tiled=True)]
    all_to_all x1 -> x0, blocking collectives: 11.9 us -> none  [per_device(): lax.all_to_all(send_panel, 'pop', split_axis=0, concat_axis=0, tiled=True)]
    dot_general x8, matrix products: 14.8 us -> 24.6 us  [one_group(): jnp.einsum('abrq,bqc->arc', high_part, group_panel, preferred_element_typ...]
    dot_general x8, matrix products: 13.6 us -> 5.98 us  [one_group(): jnp.einsum('abrq,bqc->arc', low_part, group_panel, preferred_element_type...]
    all_gather x1, waiting for transfers between devices: 3.46 us -> 9.8 us  [per_device(): lax.all_gather(tile_weights, 'site', axis=0, tiled=True)]
  transfers between devices with their start and end apart: 5 -> 6, of which waited for: 5 -> 5; matrix products, arithmetic and copies ran while one was open for 8% -> 8% of each run, Pallas kernels for 0% -> 0%
where the time goes in v1:
time: 228 us; the launch traced here: 227 us
  blocking collectives  53.4 us (23%)
  local copies, waits for them, and re-layouts  47.9 us (21%)
  matrix products  38.6 us (17%)
  starting transfers between devices  33 us (14%)
  waiting for transfers between devices  29.5 us (13%)
  between operations  14.4 us (6%)
  other arithmetic  10 us (4%)
    unnamed x1, blocking collectives  53.4 us
    dot_general x8, matrix products, one_group(): jnp.einsum('abrq,bqc->arc', high_part, group_panel, preferred_element_typ...  24.6 us
    while x16, local copies, waits for them, and re-layouts  15.3 us
    all_gather x1, waiting for transfers between devices, per_device(): lax.all_gather(tile_weights, 'site', axis=0, tiled=True)  9.8 us
    all_to_all x1, starting transfers between devices, per_device(): lax.all_to_all(send_rows, 'pop', split_axis=0, concat_axis=0, tiled=True)  8.59 us
    all_to_all x1, waiting for transfers between devices, per_device(): lax.all_to_all(sent_back, 'pop', split_axis=0, concat_axis=0, tiled=True)  8.32 us
    all_to_all x1, starting transfers between devices, gather_by_exchange(): return lax.all_to_all(copies, axis, dim, dim, tiled=True)  8.19 us
    dynamic_slice x16, local copies, waits for them, and re-layouts, pair_terms(): result_sum, unused = lax.scan(one_group, running, grouped)  7.75 us
  transfers between devices with their start and end apart: 6, of which 5 were waited for; matrix products, arithmetic and copies ran while one was open for 8% of the time, Pallas kernels for 0%

profile of v1, /device:TPU:1, one launch (start us, length us, event | category | flops | bytes accessed | tf_op | source)
XLA Modules:
  0.0 227.2 jit_solution(15145794949303971905)
XLA Ops:
  7.2 1.2 reduce-window.6
  10.1 2.6 %scatter_custom_fusion = s32[768]{0:T(1024)S(1)} fusion(s32[512]{0:T(512)S(1)} %compare_select_fusion.3, s32[512]{0:T(512)} %param.14, s32[]{:T(128)} %constant.8.clone.1), kind=kCustom, calls=%fused_computation.79 | custom fusion | bytes 3584 | tf_op jit(solution)/shard_map/scatter | solution.py:80
  13.4 8.6 %all-to-all-start = ((s32[32,1,24]{2,1,0:T(1,128)}), s32[32,1,24]{2,1,0:T(1,128)S(1)}, u32[]{:S(2)}, u32[]{:S(2)}) async-start(s32[32,1,24]{2,1,0:T(1,128)} %bitcast.2), calls=%async_computation | async-start | bytes 32768 | tf_op jit(solution)/shard_map/all_to_all | solution.py:86
  22.7 6.2 %all-to-all-done = s32[32,1,24]{2,1,0:T(1,128)S(1)} async-done(((s32[32,1,24]{2,1,0:T(1,128)}), s32[32,1,24]{2,1,0:T(1,128)S(1)}, u32[]{:S(2)}, u32[]{:S(2)}) %all-to-all-start) | async-done | bytes 3104 | tf_op jit(solution)/shard_map/all_to_all | solution.py:86
  30.2 3.6 %scatter_custom_fusion.3 = bf16[768,128]{1,0:T(8,128)(2,1)} fusion(s32[512]{0:T(512)S(1)} %compare_select_fusion.3, bf16[128,128]{1,0:T(8,128)(2,1)S(1)} %copy-done, s32[1024]{0:T(1024)S(1)} %get-tuple-element.105, bf16[]{:T(256)} %constant.19.clone.1), kind=kCustom, calls=%fused_computation.41 | custom fusion | bytes 196610 | tf_op jit(solution)/shard_map/scatter | solution.py:74
  33.9 4.2 %all-to-all-start.2 = ((bf16[32,24,128]{2,1,0:T(8,128)(2,1)}), bf16[32,24,128]{2,1,0:T(8,128)(2,1)S(1)}, u32[]{:S(2)}, u32[]{:S(2)}) async-start(bf16[32,24,128]{2,1,0:T(8,128)(2,1)} %bitcast.8), calls=%async_computation.2 | async-start | bytes 393216 | tf_op jit(solution)/shard_map/all_to_all | solution.py:85
  39.7 3.9 %scatter_custom_fusion.1 = bf16[768,96]{1,0:T(8,128)(2,1)} fusion(s32[512]{0:T(512)S(1)} %compare_select_fusion.3, s32[512]{0:T(512)S(1)} %add_minimum_fusion, s32[512]{0:T(512)} %param.15, bf16[]{:T(256)} %constant.19.clone.1, bf16[128,96]{1,0:T(8,128)(2,1)S(1)} %copy.29, s32[1024]{0:T(1024)S(1)} %get-tuple-element.105), kind=kCustom, calls=%fused_computation.40 | custom fusion | flops 196608 | bytes 189440 | tf_op jit(solution)/shard_map/scatter | solution.py:68
  43.6 2.9 %all-to-all-done.2 = bf16[32,24,128]{2,1,0:T(8,128)(2,1)S(1)} async-done(((bf16[32,24,128]{2,1,0:T(8,128)(2,1)}), bf16[32,24,128]{2,1,0:T(8,128)(2,1)S(1)}, u32[]{:S(2)}, u32[]{:S(2)}) %all-to-all-start.2) | async-done | bytes 196640 | tf_op jit(solution)/shard_map/all_to_all | solution.py:85
  46.5 4.7 %all-to-all-start.1 = ((bf16[32,24,96]{2,1,0:T(8,128)(2,1)}), bf16[32,24,96]{2,1,0:T(8,128)(2,1)S(1)}, u32[]{:S(2)}, u32[]{:S(2)}) async-start(bf16[32,24,96]{2,1,0:T(8,128)(2,1)} %bitcast.3), calls=%async_computation.1 | async-start | bytes 393216 | tf_op jit(solution)/shard_map/all_to_all | solution.py:84
  51.1 4.3 %scatter_custom_fusion.4 = bf16[1024,128]{1,0:T(8,128)(2,1)S(1)} fusion(s32[768]{0:T(1024)S(1)} %fusion.39, bf16[768,128]{1,0:T(8,128)(2,1)S(1)} %bitcast.116, bf16[]{:T(256)} %constant.19.clone.1), kind=kCustom, calls=%fused_computation.43 | custom fusion | bytes 262146 | tf_op jit(solution)/shard_map/scatter | solution.py:98
  55.8 1.3 copy-done.2
  57.2 2.3 %all-to-all-done.1 = bf16[32,24,96]{2,1,0:T(8,128)(2,1)S(1)} async-done(((bf16[32,24,96]{2,1,0:T(8,128)(2,1)}), bf16[32,24,96]{2,1,0:T(8,128)(2,1)S(1)}, u32[]{:S(2)}, u32[]{:S(2)}) %all-to-all-start.1) | async-done | bytes 147488 | tf_op jit(solution)/shard_map/all_to_all | solution.py:84
  59.5 8.2 %all-to-all-start.3 = ((bf16[64,128,128]{2,1,0:T(8,128)(2,1)}), bf16[64,128,128]{2,1,0:T(8,128)(2,1)S(1)}, u32[]{:S(2)}, u32[]{:S(2)}) async-start(bf16[64,128,128]{2,1,0:T(8,128)(2,1)} %copy-done.2), calls=%async_computation.3 | async-start | bytes 4194304 | tf_op jit(solution)/shard_map/all_to_all | solution.py:10
  67.9 4.3 %scatter_custom_fusion.2 = bf16[1024,96]{1,0:T(8,128)(2,1)S(1)} fusion(s32[768]{0:T(1024)S(1)} %fusion.39, bf16[768,96]{1,0:T(8,128)(2,1)S(1)} %bitcast.115, bf16[]{:T(256)} %constant.19.clone.1), kind=kCustom, calls=%fused_computation.47 | custom fusion | bytes 196610 | tf_op jit(solution)/shard_map/scatter | solution.py:92
  74.7 53.4 %all-reduce = s32[64]{0:T(128)S(1)} all-reduce(s32[64]{0:T(128)S(1)} %dynamic-update-slice), channel_id=1, replica_groups=mesh['pop'=32,'site'=8] {'site'}, use_global_device_ids=true, to_apply=%add | all-reduce | flops 64 | bytes 512
  128.3 9.8 %all-gather.2.cloned.1.call-done = bf16[64,128,96]{1,0,2:T(8,128)(2,1)} async-done(((bf16[8,128,96]{1,0,2:T(8,128)(2,1)}), bf16[64,128,96]{1,0,2:T(8,128)(2,1)}) %all-gather.2.cloned.1.call-update) | async-done | bytes 1572880 | tf_op jit(solution)/shard_map/all_gather | solution.py:107
  138.1 62.0 %while.11 = (s32[]{:T(128)}, f32[8,128,128]{2,1,0:T(8,128)S(1)}, bf16[8,8,128,96]{2,1,0,3:T(8,128)(2,1)}, s32[8]{0:T(128)S(1)}, s32[8,8]{1,0:T(8,128)S(1)}, /*in...) while((s32[]{:T(128)}, f32[8,128,128]{2,1,0:T(8,128)S(1)}, ...), condition=%wide.region_9.10_spmd.clone, body=%wide.region_8.9_spmd.clone.sunk | while | flops 743571584 | bytes 33161744 | solution.py:41
  138.2 0.9 constant_dynamic-slice_fusion.3
  139.2 0.9 fusion.66
  140.1 1.9 copy-done.1
  142.8 3.1 %fusion.68 = f32[8,128,128]{2,1,0:T(8,128)S(1)} fusion(f32[8,128,128]{2,1,0:T(8,128)S(1)} %fusion.67, f32[8,128,128]{2,1,0:T(8,128)S(1)} %get-tuple-element.159, pred[]{:T(512)S(6)} %compare.3, bf16[8,8,128,128]{3,2,1,0:T(8,128)(2,1)S(1)} %get-tuple-element.173, s32[]{:T(128)} %get-tuple-element.158, f32[8,8,128,128]{3,2,1,0:T(8,128)} %copy-done.1), kind=kOutput, calls=%fused_computation.18.clone.1 | convolution fusion | flops 268828672 | bytes 6029317 | tf_op jit(solution)/shard_map/while/body/eval_jaxpr/abrq,bqc->arc/dot_general | solution.py:33
  146.0 0.9 constant_dynamic-slice_fusion.3
  147.9 1.9 copy-done.1
  150.5 3.1 %fusion.68 = f32[8,128,128]{2,1,0:T(8,128)S(1)} fusion(f32[8,128,128]{2,1,0:T(8,128)S(1)} %fusion.67, f32[8,128,128]{2,1,0:T(8,128)S(1)} %get-tuple-element.159, pred[]{:T(512)S(6)} %compare.3, bf16[8,8,128,128]{3,2,1,0:T(8,128)(2,1)S(1)} %get-tuple-element.173, s32[]{:T(128)} %get-tuple-element.158, f32[8,8,128,128]{3,2,1,0:T(8,128)} %copy-done.1), kind=kOutput, calls=%fused_computation.18.clone.1 | convolution fusion | flops 268828672 | bytes 6029317 | tf_op jit(solution)/shard_map/while/body/eval_jaxpr/abrq,bqc->arc/dot_general | solution.py:33
  153.7 0.9 constant_dynamic-slice_fusion.3
  155.6 1.9 copy-done.1
  158.3 3.1 %fusion.68 = f32[8,128,128]{2,1,0:T(8,128)S(1)} fusion(f32[8,128,128]{2,1,0:T(8,128)S(1)} %fusion.67, f32[8,128,128]{2,1,0:T(8,128)S(1)} %get-tuple-element.159, pred[]{:T(512)S(6)} %compare.3, bf16[8,8,128,128]{3,2,1,0:T(8,128)(2,1)S(1)} %get-tuple-element.173, s32[]{:T(128)} %get-tuple-element.158, f32[8,8,128,128]{3,2,1,0:T(8,128)} %copy-done.1), kind=kOutput, calls=%fused_computation.18.clone.1 | convolution fusion | flops 268828672 | bytes 6029317 | tf_op jit(solution)/shard_map/while/body/eval_jaxpr/abrq,bqc->arc/dot_general | solution.py:33
  161.5 0.9 constant_dynamic-slice_fusion.3
  163.4 1.9 copy-done.1
  166.0 3.1 %fusion.68 = f32[8,128,128]{2,1,0:T(8,128)S(1)} fusion(f32[8,128,128]{2,1,0:T(8,128)S(1)} %fusion.67, f32[8,128,128]{2,1,0:T(8,128)S(1)} %get-tuple-element.159, pred[]{:T(512)S(6)} %compare.3, bf16[8,8,128,128]{3,2,1,0:T(8,128)(2,1)S(1)} %get-tuple-element.173, s32[]{:T(128)} %get-tuple-element.158, f32[8,8,128,128]{3,2,1,0:T(8,128)} %copy-done.1), kind=kOutput, calls=%fused_computation.18.clone.1 | convolution fusion | flops 268828672 | bytes 6029317 | tf_op jit(solution)/shard_map/while/body/eval_jaxpr/abrq,bqc->arc/dot_general | solution.py:33
  169.2 0.9 constant_dynamic-slice_fusion.3
  171.1 1.9 copy-done.1
  173.8 3.1 %fusion.68 = f32[8,128,128]{2,1,0:T(8,128)S(1)} fusion(f32[8,128,128]{2,1,0:T(8,128)S(1)} %fusion.67, f32[8,128,128]{2,1,0:T(8,128)S(1)} %get-tuple-element.159, pred[]{:T(512)S(6)} %compare.3, bf16[8,8,128,128]{3,2,1,0:T(8,128)(2,1)S(1)} %get-tuple-element.173, s32[]{:T(128)} %get-tuple-element.158, f32[8,8,128,128]{3,2,1,0:T(8,128)} %copy-done.1), kind=kOutput, calls=%fused_computation.18.clone.1 | convolution fusion | flops 268828672 | bytes 6029317 | tf_op jit(solution)/shard_map/while/body/eval_jaxpr/abrq,bqc->arc/dot_general | solution.py:33
  177.0 0.9 constant_dynamic-slice_fusion.3
  178.9 1.9 copy-done.1
  181.6 3.1 %fusion.68 = f32[8,128,128]{2,1,0:T(8,128)S(1)} fusion(f32[8,128,128]{2,1,0:T(8,128)S(1)} %fusion.67, f32[8,128,128]{2,1,0:T(8,128)S(1)} %get-tuple-element.159, pred[]{:T(512)S(6)} %compare.3, bf16[8,8,128,128]{3,2,1,0:T(8,128)(2,1)S(1)} %get-tuple-element.173, s32[]{:T(128)} %get-tuple-element.158, f32[8,8,128,128]{3,2,1,0:T(8,128)} %copy-done.1), kind=kOutput, calls=%fused_computation.18.clone.1 | convolution fusion | flops 268828672 | bytes 6029317 | tf_op jit(solution)/shard_map/while/body/eval_jaxpr/abrq,bqc->arc/dot_general | solution.py:33
  184.7 0.9 constant_dynamic-slice_fusion.3
  185.7 0.9 fusion.66
  186.6 1.9 copy-done.1
  189.3 3.1 %fusion.68 = f32[8,128,128]{2,1,0:T(8,128)S(1)} fusion(f32[8,128,128]{2,1,0:T(8,128)S(1)} %fusion.67, f32[8,128,128]{2,1,0:T(8,128)S(1)} %get-tuple-element.159, pred[]{:T(512)S(6)} %compare.3, bf16[8,8,128,128]{3,2,1,0:T(8,128)(2,1)S(1)} %get-tuple-element.173, s32[]{:T(128)} %get-tuple-element.158, f32[8,8,128,128]{3,2,1,0:T(8,128)} %copy-done.1), kind=kOutput, calls=%fused_computation.18.clone.1 | convolution fusion | flops 268828672 | bytes 6029317 | tf_op jit(solution)/shard_map/while/body/eval_jaxpr/abrq,bqc->arc/dot_general | solution.py:33
  192.5 0.9 constant_dynamic-slice_fusion.3
  193.5 0.9 fusion.66
  194.4 1.9 copy-done.1
  197.1 3.1 %fusion.68 = f32[8,128,128]{2,1,0:T(8,128)S(1)} fusion(f32[8,128,128]{2,1,0:T(8,128)S(1)} %fusion.67, f32[8,128,128]{2,1,0:T(8,128)S(1)} %get-tuple-element.159, pred[]{:T(512)S(6)} %compare.3, bf16[8,8,128,128]{3,2,1,0:T(8,128)(2,1)S(1)} %get-tuple-element.173, s32[]{:T(128)} %get-tuple-element.158, f32[8,8,128,128]{3,2,1,0:T(8,128)} %copy-done.1), kind=kOutput, calls=%fused_computation.18.clone.1 | convolution fusion | flops 268828672 | bytes 6029317 | tf_op jit(solution)/shard_map/while/body/eval_jaxpr/abrq,bqc->arc/dot_general | solution.py:33
  200.2 2.5 %gather_fusion = bf16[768,128]{1,0:T(8,128)(2,1)} fusion(bf16[1024,128]{1,0:T(8,128)(2,1)S(1)} %bitcast.109, s32[1024]{0:T(1024)S(1)} %get-tuple-element.104), kind=kCustom, calls=%fused_computation.2 | custom fusion | bytes 396288 | tf_op jit(solution)/shard_map/gather | solution.py:113
  202.7 7.1 %all-to-all-start.4 = ((bf16[32,24,128]{2,1,0:T(8,128)(2,1)}), bf16[32,24,128]{2,1,0:T(8,128)(2,1)S(1)}, u32[]{:S(2)}, u32[]{:S(2)}) async-start(bf16[32,24,128]{2,1,0:T(8,128)(2,1)} %bitcast.14), calls=%async_computation.4 | async-start | bytes 393216 | tf_op jit(solution)/shard_map/all_to_all | solution.py:114
  209.9 8.3 %all-to-all-done.4 = bf16[32,24,128]{2,1,0:T(8,128)(2,1)S(1)} async-done(((bf16[32,24,128]{2,1,0:T(8,128)(2,1)}), bf16[32,24,128]{2,1,0:T(8,128)(2,1)S(1)}, u32[]{:S(2)}, u32[]{:S(2)}) %all-to-all-start.4) | async-done | bytes 196640 | tf_op jit(solution)/shard_map/all_to_all | solution.py:114
  218.2 1.3 gather_fusion.1
  (92 shorter events, 21.5 us)
Async XLA Ops:
  6.5 23.7 %copy-start = (bf16[128,128]{1,0:T(8,128)(2,1)S(1)}, bf16[128,128]{1,0:T(8,128)(2,1)}, u32[]{:S(2)}) copy-start(bf16[128,128]{1,0:T(8,128)(2,1)} %param.11) | copy-start | bytes 98308
  13.4 15.5 %all-to-all-start = ((s32[32,1,24]{2,1,0:T(1,128)}), s32[32,1,24]{2,1,0:T(1,128)S(1)}, u32[]{:S(2)}, u32[]{:S(2)}) async-start(s32[32,1,24]{2,1,0:T(1,128)} %bitcast.2), calls=%async_computation | async-start | bytes 32768 | tf_op jit(solution)/shard_map/all_to_all | solution.py:86
  33.9 12.6 %all-to-all-start.2 = ((bf16[32,24,128]{2,1,0:T(8,128)(2,1)}), bf16[32,24,128]{2,1,0:T(8,128)(2,1)S(1)}, u32[]{:S(2)}, u32[]{:S(2)}) async-start(bf16[32,24,128]{2,1,0:T(8,128)(2,1)} %bitcast.8), calls=%async_computation.2 | async-start | bytes 393216 | tf_op jit(solution)/shard_map/all_to_all | solution.py:85
  46.5 13.0 %all-to-all-start.1 = ((bf16[32,24,96]{2,1,0:T(8,128)(2,1)}), bf16[32,24,96]{2,1,0:T(8,128)(2,1)S(1)}, u32[]{:S(2)}, u32[]{:S(2)}) async-start(bf16[32,24,96]{2,1,0:T(8,128)(2,1)} %bitcast.3), calls=%async_computation.1 | async-start | bytes 393216 | tf_op jit(solution)/shard_map/all_to_all | solution.py:84
  55.8 1.4 copy-start.2
  57.1 15.9 %copy-start.5 = (u32[256]{0:T(256)S(1)}, u32[256]{0:T(256)}, u32[]{:S(2)}) copy-start(u32[256]{0:T(256)} %constant.52) | copy-start | bytes 3076
  57.1 17.3 %copy-start.3 = (s32[8]{0:T(128)S(1)}, s32[8]{0:T(128)}, u32[]{:S(2)}) copy-start(s32[8]{0:T(128)} %param.17) | copy-start | bytes 100
  59.5 78.7 %all-to-all-start.3 = ((bf16[64,128,128]{2,1,0:T(8,128)(2,1)}), bf16[64,128,128]{2,1,0:T(8,128)(2,1)S(1)}, u32[]{:S(2)}, u32[]{:S(2)}) async-start(bf16[64,128,128]{2,1,0:T(8,128)(2,1)} %copy-done.2), calls=%async_computation.3 | async-start | bytes 4194304 | tf_op jit(solution)/shard_map/all_to_all | solution.py:10
  67.7 70.5 %all-gather.2.cloned.1.call-start = ((), (), s32[]{:S(2)}) async-start(), calls=%async_computation.5 | async-start | bytes 1769472 | tf_op jit(solution)/shard_map/all_gather | solution.py:107
  140.1 1.9 copy-start.1
  147.9 1.9 copy-start.1
  155.6 1.9 copy-start.1
  163.4 1.9 copy-start.1
  171.1 1.9 copy-start.1
  178.9 1.9 copy-start.1
  186.6 1.9 copy-start.1
  194.4 1.9 copy-start.1
  200.1 19.4 %copy-start.4 = (s32[512]{0:T(512)S(1)}, s32[512]{0:T(512)}, u32[]{:S(2)}) copy-start(s32[512]{0:T(512)} %param.12) | copy-start | bytes 6148
  202.7 15.5 %all-to-all-start.4 = ((bf16[32,24,128]{2,1,0:T(8,128)(2,1)}), bf16[32,24,128]{2,1,0:T(8,128)(2,1)S(1)}, u32[]{:S(2)}, u32[]{:S(2)}) async-start(bf16[32,24,128]{2,1,0:T(8,128)(2,1)} %bitcast.14), calls=%async_computation.4 | async-start | bytes 393216 | tf_op jit(solution)/shard_map/all_to_all | solution.py:114
Sparse Core Ops, SparseCore 0:
  73.2 64.8 all-gather.1
